TPU v7x, 32 devices: a whole 2x2x4 slice. The times are simulated.
32 devices in a mesh: rows: 16 (over z, y, x), trees: 2 (over core).
Axes of the slice: x: 2, y: 2, z: 4, core: 2. Of those that a mesh axis runs over, the one named last changes fastest.
Arguments:
- tiles: bfloat16 [2, 16, 4, 256, 256], P('trees', 'rows'), may hold values from -0.0625 to 0.0625
- tile_src: int32 [2, 16, 4], P('trees', 'rows'), may hold values from 0 to 3, as said below
- tile_dst: int32 [2, 16, 4], P('trees', 'rows'), may hold values from 0 to 1
- leaf_rhs: bfloat16 [2, 16, 256, 128], P('trees', 'rows'), may hold values from -6 to 6
- leaf_inv: bfloat16 [2, 16, 256, 256], P('trees', 'rows'), may hold values from -0.375 to 0.375
- leaf_owner: int32 [2, 2], P('trees'), may hold values from 0 to 15, as said below
- anc_rhs: bfloat16 [2, 16, 256, 128], P('trees', 'rows'), may hold values from -5 to 5
- anc_inv: bfloat16 [16, 256, 256], P('rows'), may hold values from -0.25 to 0.25
- anc_owner: int32 [4], replicated, may hold values from 0 to 15, as said below
Outputs:
- solved: bfloat16 [4, 256, 128], P(None, None, 'rows')
Inputs may be any that keep to these rules, and one draw needn't show every extreme that they name: `leaf_owner`: the 2 owners of one subtree differ. `anc_owner`: all owners differ. `tile_src`: a tile of wave w names a block below 2 * w.
All inputs are finite; a program needn't handle non-finite values.
Results may differ from a plain program's by a relative error of at most 0.011.
Values may be sent and summed in bfloat16 or wider, within the bound.
A program may use at most 64 MiB of HBM per device.

v0:
```python
import functools

import jax
import jax.numpy as jnp
from jax import lax
from jax.experimental import pallas as pl
from jax.experimental.pallas import tpu as pltpu
from jax.sharding import PartitionSpec as P

WAVES = 3
WB = 2
TW = 2
MESH = pl.DeviceIdType.MESH
F32 = jnp.float32
BF16 = jnp.bfloat16


def broadcast(block, axis, source):
    block = jnp.where(lax.axis_index(axis) == source, block, jnp.zeros_like(block))
    return lax.psum(block, axis)


def general_body(tiles, tile_src, tile_dst, leaf_rhs, leaf_inv, leaf_owner, anc_rhs, anc_inv, anc_owner):
    row_count = lax.axis_size("rows")
    here = lax.axis_index("rows")
    share = leaf_rhs.shape[-1] // row_count
    own_leaf = jnp.dot(leaf_inv[0, 0], leaf_rhs[0, 0], preferred_element_type=F32).astype(BF16)
    known = []
    for block in range(WB):
        known.append(broadcast(own_leaf, "rows", leaf_owner[0, block]))
    outputs = []
    for wave in range(1, WAVES):
        start = (wave - 1) * TW
        sources = jnp.stack(known)
        block_tiles = tiles[0, 0, start : start + TW]
        picked = jnp.take(sources, tile_src[0, 0, start : start + TW], axis=0)
        product = jnp.einsum("kij,kjr->kir", block_tiles, picked, preferred_element_type=F32)
        onehot = (
            tile_dst[0, 0, start : start + TW][:, None] == jnp.arange(WB, dtype=jnp.int32)[None, :]
        ).astype(F32)
        owners = anc_owner[(wave - 1) * WB : wave * WB]
        mine = (owners == here).astype(F32)
        partial_value = mine[:, None, None] * anc_rhs[0, 0].astype(F32)[None] - jnp.einsum(
            "kb,kir->bir", onehot, product
        )
        summed = lax.psum(partial_value, ("rows", "trees"))
        chosen = jnp.einsum("b,bir->ir", mine, summed).astype(BF16)
        local_x = jnp.dot(anc_inv[0], chosen, preferred_element_type=F32).astype(BF16)
        for block in range(WB):
            result = broadcast(local_x, "rows", owners[block])
            known.append(result)
            outputs.append(lax.dynamic_slice_in_dim(result, here * share, share, 1))
    return jnp.stack(outputs)


NT = (((1,), (1,)), ((), ()))


def kernel(
    n, nt, tiles_h, src, dst, rhs_h, linv_h, lown, arhs_h, ainv_h, aown, out,
    tiles, rhs, linv, arhs, ainv, own, leaf_rs, leaf_ag, inv_rs, inv_ag, known, u_send, u_recv, xs,
    lsem, ssem, rsem,
):
    r = lax.axis_index("rows")
    t = lax.axis_index("trees")
    depth = rhs.shape[0]
    count = rhs.shape[1]
    ch = depth // n
    share = count // n
    every = n * nt

    def peer(k):
        flat = lax.rem(r * nt + t + k, every)
        return flat // nt, lax.rem(flat, nt)

    barrier = pltpu.get_barrier_semaphore()

    @pl.loop(1, every)
    def _(k):
        pr, pt = peer(k)
        pl.semaphore_signal(barrier, inc=1, device_id=(pr, pt), device_id_type=MESH)

    loads = []
    for i, (a, b) in enumerate(
        ((linv_h.at[0, 0], linv), (rhs_h.at[0, 0], rhs), (ainv_h.at[0], ainv), (arhs_h.at[0, 0], arhs), (tiles_h.at[0, 0], tiles))
    ):
        c = pltpu.make_async_copy(a, b, lsem.at[i])
        c.start()
        loads.append(c)
    loads[0].wait()
    loads[1].wait()
    own_leaf = jnp.dot(linv[...], rhs[...], preferred_element_type=F32).astype(BF16)
    own[...] = own_leaf.reshape(n, ch, count)
    loads[2].wait()
    pl.semaphore_wait(barrier, every - 1)

    def rows_send(phase, make):
        @pl.loop(1, n)
        def _(k):
            j = lax.rem(r + k, n)
            a, b = make(j)
            pltpu.make_async_remote_copy(
                src_ref=a, dst_ref=b, send_sem=ssem.at[phase], recv_sem=rsem.at[phase],
                device_id=(j, t), device_id_type=MESH,
            ).start()

    def all_send(phase, make):
        @pl.loop(1, every)
        def _(k):
            pr, pt = peer(k)
            a, b = make(pr, pt)
            pltpu.make_async_remote_copy(
                src_ref=a, dst_ref=b, send_sem=ssem.at[phase], recv_sem=rsem.at[phase],
                device_id=(pr, pt), device_id_type=MESH,
            ).start()

    def landed(phase, view):
        pltpu.make_async_copy(view, view, rsem.at[phase]).wait()

    def sent(phase, view):
        pltpu.make_async_copy(view, view, ssem.at[phase]).wait()

    most = pl.ds(0, n - 1)
    rows_send(0, lambda j: (own.at[j], leaf_rs.at[r]))
    leaf_rs[r] = own[r]
    rows_send(1, lambda j: (ainv.at[pl.ds(pl.multiple_of(j * ch, ch), ch)], inv_rs.at[r]))
    inv_rs[r] = ainv[pl.ds(pl.multiple_of(r * ch, ch), ch), :]

    landed(0, leaf_rs.at[most])
    for b in range(WB):
        leaf_ag[r, b] = leaf_rs[lown[0, b]]
    rows_send(2, lambda j: (leaf_ag.at[r], leaf_ag.at[r]))
    landed(1, inv_rs.at[most])
    for w in range(WAVES - 1):
        inv_ag[w, r] = inv_rs[aown[w * WB + t]]
    rows_send(3, lambda j: (inv_ag.at[0, r], inv_ag.at[0, r]))

    loads[3].wait()
    loads[4].wait()
    arhs_t = arhs[...].astype(F32).T
    landed(2, leaf_ag.at[most])
    for b in range(WB):
        known[b] = leaf_ag[:, b].reshape(depth, count).astype(F32).T.astype(BF16)

    for w in range(WAVES - 1):
        up = 4 + 3 * w
        products = []
        for k in range(w * TW, (w + 1) * TW):
            products.append(
                lax.dot_general(known[src[0, 0, k]], tiles[k], NT, preferred_element_type=F32)
            )
        for b in range(WB):
            part = jnp.where(aown[w * WB + b] == r, arhs_t, 0.0)
            for k in range(TW):
                part = part - jnp.where(dst[0, 0, w * TW + k] == b, products[k], 0.0)
            u_send[w, b] = part.reshape(n, share, depth).astype(BF16)
        all_send(up, lambda pr, pt: (u_send.at[w, pt, pr], u_recv.at[w, r * nt + t]))
        u_recv[w, r * nt + t] = u_send[w, t, r]
        if w + 1 < WAVES - 1:
            rows_send(up + 1, lambda j: (inv_ag.at[w + 1, r], inv_ag.at[w + 1, r]))
        landed(up, u_recv.at[w, pl.ds(0, every - 1)])
        y = jnp.sum(u_recv[w].astype(F32), axis=0).astype(BF16)
        landed(3 if w == 0 else 4 + 3 * (w - 1) + 1, inv_ag.at[w, most])
        inv = inv_ag[w].reshape(depth, depth)
        x = lax.dot_general(y, inv, NT, preferred_element_type=F32).astype(BF16)
        xs[w, t, r] = x
        if w + 1 < WAVES - 1:
            all_send(up + 2, lambda pr, pt: (xs.at[w, t, r], xs.at[w, t, r]))
            landed(up + 2, u_recv.at[w, pl.ds(0, every - 1)])
            for b in range(WB):
                known[(w + 1) * WB + b] = xs[w, b].reshape(count, depth)
        else:
            last = up + 1
            pltpu.make_async_remote_copy(
                src_ref=xs.at[w, t, r], dst_ref=xs.at[w, t, r], send_sem=ssem.at[last],
                recv_sem=rsem.at[last], device_id=(r, 1 - t), device_id_type=MESH,
            ).start()
            landed(last, xs.at[w, 0, 0])
    for w in range(WAVES - 1):
        for b in range(WB):
            out[w * WB + b] = xs[w, b, r]

    sent(0, own.at[most])
    sent(1, inv_rs.at[most])
    sent(2, leaf_ag.at[most])
    sent(3, inv_ag.at[0, most])
    for w in range(WAVES - 1):
        up = 4 + 3 * w
        sent(up, u_recv.at[w, pl.ds(0, every - 1)])
        if w + 1 < WAVES - 1:
            sent(up + 1, inv_ag.at[w + 1, most])
            sent(up + 2, u_recv.at[w, pl.ds(0, every - 1)])
        else:
            sent(up + 1, xs.at[w, 0, 0])


def fast_body(n, nt, tiles, tile_src, tile_dst, leaf_rhs, leaf_inv, leaf_owner, anc_rhs, anc_inv, anc_owner):
    depth, count = leaf_rhs.shape[-2:]
    kinds = tiles.shape[2]
    ch, share, every = depth // n, count // n, n * nt
    waves = WAVES - 1
    phases = 4 + 3 * waves
    any_spec = pl.BlockSpec(memory_space=pl.ANY)
    smem = pl.BlockSpec(memory_space=pltpu.SMEM)
    found = pl.pallas_call(
        functools.partial(kernel, n, nt),
        out_shape=jax.ShapeDtypeStruct((waves * WB, share, depth), BF16),
        in_specs=[any_spec, smem, smem, any_spec, any_spec, smem, any_spec, any_spec, smem],
        out_specs=pl.BlockSpec(memory_space=pltpu.VMEM),
        scratch_shapes=[
            pltpu.VMEM((kinds, depth, depth), BF16),
            pltpu.VMEM((depth, count), BF16),
            pltpu.VMEM((depth, depth), BF16),
            pltpu.VMEM((depth, count), BF16),
            pltpu.VMEM((depth, depth), BF16),
            pltpu.VMEM((n, ch, count), BF16),
            pltpu.VMEM((n, ch, count), BF16),
            pltpu.VMEM((n, WB, ch, count), BF16),
            pltpu.VMEM((n, ch, depth), BF16),
            pltpu.VMEM((waves, n, ch, depth), BF16),
            pltpu.VMEM((WB * waves, count, depth), BF16),
            pltpu.VMEM((waves, WB, n, share, depth), BF16),
            pltpu.VMEM((waves, every, share, depth), BF16),
            pltpu.VMEM((waves, WB, n, share, depth), BF16),
            pltpu.SemaphoreType.DMA((5,)),
            pltpu.SemaphoreType.DMA((phases,)),
            pltpu.SemaphoreType.DMA((phases,)),
        ],
        compiler_params=pltpu.CompilerParams(collective_id=0, has_side_effects=True),
    )(tiles, tile_src, tile_dst, leaf_rhs, leaf_inv, leaf_owner, anc_rhs, anc_inv, anc_owner)
    return jnp.swapaxes(found, 1, 2)


def solution(mesh):
    n, nt = mesh.shape["rows"], mesh.shape["trees"]
    placed = (
        P("trees", "rows", None, None, None),
        P("trees", "rows", None),
        P("trees", "rows", None),
        P("trees", "rows", None, None),
        P("trees", "rows", None, None),
        P("trees", None),
        P("trees", "rows", None, None),
        P("rows", None, None),
        P(),
    )

    def body(*args):
        depth, count = args[3].shape[-2:]
        if nt == WB and depth % (16 * n) == 0 and count % (8 * n) == 0:
            return fast_body(n, nt, *args)
        return general_body(*args)

    return jax.shard_map(
        body, mesh=mesh, in_specs=placed, out_specs=P(None, None, "rows"), check_vma=False
    )
```

profile of v0, /device:TPU:0, one launch (start us, length us, event | category | flops | bytes accessed | tf_op | source)
XLA Modules:
  0.0 39.0 jit_solution(6921432184599623113)
XLA Ops:
  0.0 37.7 %shard_map.91 = bf16[4,8,256]{2,1,0:T(8,128)(2,1)} custom-call(bf16[1,1,4,256,256]{4,3,2,1,0:T(8,128)(2,1)} %tiles_h.1, s32[1,1,4]{2,1,0:T(1,128)} %src.1, s32[1,1,4]{2,1,0:T(1,128)} %dst.1, bf16[1,1,256,128]{3,2,1,0:T(8,128)(2,1)} %rhs_h.1, bf16[1,1,256,256]{3,2,1,0:T(8,128)(2,1)} %linv_h.1, s32[1,2]{1,0:T(1,128)} %lown.1, bf16[1,1,256,128]{3,2,1,0:T(8,128)(2,1)} %arhs_h.1, ...), custom_call_target="tpu_custom_call" | custom-call | tf_op jit(solution)/shard_map/pallas_call | solution.py:205
  37.7 1.3 %copy.11 = bf16[4,256,8]{1,2,0:T(8,128)(2,1)} copy(bf16[4,256,8]{1,2,0:T(8,128)(2,1)} %bitcast.1) | data formatting | bytes 32768
where the time goes:
time: 39.3 us; the launch traced here: 39 us
  Pallas kernels  37.7 us (96%)
  local copies, waits for them, and re-layouts  1.32 us (3%)
    pallas_call x1, Pallas kernels, fast_body(): pl.pallas_call(functools.partial(kernel, n, nt), out_shape=jax.ShapeDtype...  37.7 us
    unnamed x1, local copies, waits for them, and re-layouts  1.32 us

commit v1 on v0

--- a/solution.py
+++ b/solution.py
@@ -69,16 +69,23 @@
     share = count // n
     every = n * nt
 
-    def peer(k):
-        flat = lax.rem(r * nt + t + k, every)
-        return flat // nt, lax.rem(flat, nt)
+    def partner(m):
+        if n & (n - 1):
+            return lax.rem(r + m, n)
+        j = r
+        bit = 1
+        while bit < n:
+            if m & bit:
+                j = j + bit * (1 - 2 * lax.rem(r // bit, 2))
+            bit *= 2
+        return j
+
+    others = [partner(m) for m in range(n - 1, 0, -1)]
+    everyone = [(j, q) for j in others for q in (t, 1 - t)] + [(r, 1 - t)]
 
     barrier = pltpu.get_barrier_semaphore()
-
-    @pl.loop(1, every)
-    def _(k):
-        pr, pt = peer(k)
-        pl.semaphore_signal(barrier, inc=1, device_id=(pr, pt), device_id_type=MESH)
+    for where in everyone:
+        pl.semaphore_signal(barrier, inc=1, device_id=where, device_id_type=MESH)
 
     loads = []
     for i, (a, b) in enumerate(
@@ -89,15 +96,13 @@
         loads.append(c)
     loads[0].wait()
     loads[1].wait()
-    own_leaf = jnp.dot(linv[...], rhs[...], preferred_element_type=F32).astype(BF16)
-    own[...] = own_leaf.reshape(n, ch, count)
+    own_leaf = jnp.dot(linv[...], rhs[...], preferred_element_type=F32)
+    own[...] = own_leaf.T.astype(BF16).reshape(n, share, depth)
     loads[2].wait()
     pl.semaphore_wait(barrier, every - 1)
 
     def rows_send(phase, make):
-        @pl.loop(1, n)
-        def _(k):
-            j = lax.rem(r + k, n)
+        for j in others:
             a, b = make(j)
             pltpu.make_async_remote_copy(
                 src_ref=a, dst_ref=b, send_sem=ssem.at[phase], recv_sem=rsem.at[phase],
@@ -105,9 +110,7 @@
             ).start()
 
     def all_send(phase, make):
-        @pl.loop(1, every)
-        def _(k):
-            pr, pt = peer(k)
+        for pr, pt in everyone:
             a, b = make(pr, pt)
             pltpu.make_async_remote_copy(
                 src_ref=a, dst_ref=b, send_sem=ssem.at[phase], recv_sem=rsem.at[phase],
@@ -140,7 +143,7 @@
     arhs_t = arhs[...].astype(F32).T
     landed(2, leaf_ag.at[most])
     for b in range(WB):
-        known[b] = leaf_ag[:, b].reshape(depth, count).astype(F32).T.astype(BF16)
+        known[b] = leaf_ag[:, b].reshape(count, depth)
 
     for w in range(WAVES - 1):
         up = 4 + 3 * w
@@ -213,9 +216,9 @@
             pltpu.VMEM((depth, depth), BF16),
             pltpu.VMEM((depth, count), BF16),
             pltpu.VMEM((depth, depth), BF16),
-            pltpu.VMEM((n, ch, count), BF16),
-            pltpu.VMEM((n, ch, count), BF16),
-            pltpu.VMEM((n, WB, ch, count), BF16),
+            pltpu.VMEM((n, share, depth), BF16),
+            pltpu.VMEM((n, share, depth), BF16),
+            pltpu.VMEM((n, WB, share, depth), BF16),
             pltpu.VMEM((n, ch, depth), BF16),
             pltpu.VMEM((waves, n, ch, depth), BF16),
             pltpu.VMEM((WB * waves, count, depth), BF16),

time: 39.3 us -> 38.5 us (0.980)
  Pallas kernels: 37.7 us -> 36.9 us
    pallas_call x1, Pallas kernels: 37.7 us -> 36.9 us  [fast_body(): pl.pallas_call(functools.partial(kernel, n, nt), out_shape=jax.ShapeDtype...]
where the time goes in v1:
time: 38.5 us; the launch traced here: 38.3 us
  Pallas kernels  36.9 us (96%)
  local copies, waits for them, and re-layouts  1.32 us (3%)
    pallas_call x1, Pallas kernels, fast_body(): pl.pallas_call(functools.partial(kernel, n, nt), out_shape=jax.ShapeDtype...  36.9 us
    unnamed x1, local copies, waits for them, and re-layouts  1.32 us

profile of v1, /device:TPU:0, one launch (start us, length us, event | category | flops | bytes accessed | tf_op | source)
XLA Modules:
  0.0 38.3 jit_solution(5989611242754848415)
XLA Ops:
  0.0 36.9 %shard_map.91 = bf16[4,8,256]{2,1,0:T(8,128)(2,1)} custom-call(bf16[1,1,4,256,256]{4,3,2,1,0:T(8,128)(2,1)} %tiles_h.1, s32[1,1,4]{2,1,0:T(1,128)} %src.1, s32[1,1,4]{2,1,0:T(1,128)} %dst.1, bf16[1,1,256,128]{3,2,1,0:T(8,128)(2,1)} %rhs_h.1, bf16[1,1,256,256]{3,2,1,0:T(8,128)(2,1)} %linv_h.1, s32[1,2]{1,0:T(1,128)} %lown.1, bf16[1,1,256,128]{3,2,1,0:T(8,128)(2,1)} %arhs_h.1, ...), custom_call_target="tpu_custom_call" | custom-call | tf_op jit(solution)/shard_map/pallas_call | solution.py:208
  36.9 1.3 %copy.11 = bf16[4,256,8]{1,2,0:T(8,128)(2,1)} copy(bf16[4,256,8]{1,2,0:T(8,128)(2,1)} %bitcast.1) | data formatting | bytes 32768

commit v2 on v1

--- a/solution.py
+++ b/solution.py
@@ -58,7 +58,7 @@
 
 def kernel(
     n, nt, tiles_h, src, dst, rhs_h, linv_h, lown, arhs_h, ainv_h, aown, out,
-    tiles, rhs, linv, arhs, ainv, own, leaf_rs, leaf_ag, inv_rs, inv_ag, known, u_send, u_recv, xs,
+    tiles, rhs, linv, arhs, ainv, own, leaf_rs, leaf_ag, inv_rs, inv_half, inv_ag, known, u_send, u_recv, xs,
     lsem, ssem, rsem,
 ):
     r = lax.axis_index("rows")
@@ -124,10 +124,39 @@
         pltpu.make_async_copy(view, view, ssem.at[phase]).wait()
 
     most = pl.ds(0, n - 1)
+    inner = 1
+    while inner * inner * 4 <= n and n % (inner * 2) == 0:
+        inner *= 2
+    outer = n // inner
+    ro, ri = r // inner, lax.rem(r, inner)
+    chunk = ri * outer + ro
+    lanes_each = depth // nt
+    lanes = pl.ds(pl.multiple_of(t * lanes_each, lanes_each), lanes_each)
+
+    def inv_part(j):
+        at = (lax.rem(j, inner) * outer + j // inner) * ch
+        return pl.ds(pl.multiple_of(at, ch), ch)
+
+    def push(phase, a, b, where):
+        pltpu.make_async_remote_copy(
+            src_ref=a, dst_ref=b, send_sem=ssem.at[phase], recv_sem=rsem.at[phase],
+            device_id=where, device_id_type=MESH,
+        ).start()
+
+    def inner_send(w, phase):
+        held = pl.ds(ri * outer, outer)
+        for k in range(1, inner):
+            to = ro * inner + lax.rem(ri + k, inner)
+            push(phase, inv_ag.at[w, held], inv_ag.at[w, held], (to, t))
+
+    inner_view = inv_ag.at[0, pl.ds(0, (inner - 1) * outer)]
+    outer_view = inv_ag.at[0, pl.ds(0, (outer - 1) * (WAVES - 1))]
+    last = 4 + 3 * (WAVES - 1)
+    swap = last + 1
     rows_send(0, lambda j: (own.at[j], leaf_rs.at[r]))
     leaf_rs[r] = own[r]
-    rows_send(1, lambda j: (ainv.at[pl.ds(pl.multiple_of(j * ch, ch), ch)], inv_rs.at[r]))
-    inv_rs[r] = ainv[pl.ds(pl.multiple_of(r * ch, ch), ch), :]
+    rows_send(1, lambda j: (ainv.at[inv_part(j), lanes], inv_rs.at[r]))
+    inv_rs[r] = ainv[inv_part(r), lanes]
 
     landed(0, leaf_rs.at[most])
     for b in range(WB):
@@ -135,8 +164,15 @@
     rows_send(2, lambda j: (leaf_ag.at[r], leaf_ag.at[r]))
     landed(1, inv_rs.at[most])
     for w in range(WAVES - 1):
-        inv_ag[w, r] = inv_rs[aown[w * WB + t]]
-    rows_send(3, lambda j: (inv_ag.at[0, r], inv_ag.at[0, r]))
+        inv_half[w] = inv_rs[aown[w * WB + 1 - t]]
+        push(swap, inv_half.at[w], inv_ag.at[w, chunk, :, lanes], (r, 1 - t))
+    for w in range(WAVES - 1):
+        inv_ag[w, chunk, :, lanes] = inv_rs[aown[w * WB + t]]
+    landed(swap, inv_half)
+    for k in range(1, outer):
+        to = lax.rem(ro + k, outer) * inner + ri
+        for w in range(WAVES - 1):
+            push(3, inv_ag.at[w, chunk], inv_ag.at[w, chunk], (to, t))
 
     loads[3].wait()
     loads[4].wait()
@@ -159,21 +195,22 @@
             u_send[w, b] = part.reshape(n, share, depth).astype(BF16)
         all_send(up, lambda pr, pt: (u_send.at[w, pt, pr], u_recv.at[w, r * nt + t]))
         u_recv[w, r * nt + t] = u_send[w, t, r]
-        if w + 1 < WAVES - 1:
-            rows_send(up + 1, lambda j: (inv_ag.at[w + 1, r], inv_ag.at[w + 1, r]))
+        if w == 0:
+            landed(3, outer_view)
+            inner_send(0, up + 1)
         landed(up, u_recv.at[w, pl.ds(0, every - 1)])
         y = jnp.sum(u_recv[w].astype(F32), axis=0).astype(BF16)
-        landed(3 if w == 0 else 4 + 3 * (w - 1) + 1, inv_ag.at[w, most])
+        landed(up + 1, inner_view)
         inv = inv_ag[w].reshape(depth, depth)
         x = lax.dot_general(y, inv, NT, preferred_element_type=F32).astype(BF16)
         xs[w, t, r] = x
         if w + 1 < WAVES - 1:
             all_send(up + 2, lambda pr, pt: (xs.at[w, t, r], xs.at[w, t, r]))
+            inner_send(w + 1, up + 4)
             landed(up + 2, u_recv.at[w, pl.ds(0, every - 1)])
             for b in range(WB):
                 known[(w + 1) * WB + b] = xs[w, b].reshape(count, depth)
         else:
-            last = up + 1
             pltpu.make_async_remote_copy(
                 src_ref=xs.at[w, t, r], dst_ref=xs.at[w, t, r], send_sem=ssem.at[last],
                 recv_sem=rsem.at[last], device_id=(r, 1 - t), device_id_type=MESH,
@@ -186,15 +223,15 @@
     sent(0, own.at[most])
     sent(1, inv_rs.at[most])
     sent(2, leaf_ag.at[most])
-    sent(3, inv_ag.at[0, most])
+    sent(3, outer_view)
+    sent(swap, inv_half)
+    sent(last, xs.at[0, 0, 0])
     for w in range(WAVES - 1):
         up = 4 + 3 * w
         sent(up, u_recv.at[w, pl.ds(0, every - 1)])
+        sent(up + 1, inner_view)
         if w + 1 < WAVES - 1:
-            sent(up + 1, inv_ag.at[w + 1, most])
             sent(up + 2, u_recv.at[w, pl.ds(0, every - 1)])
-        else:
-            sent(up + 1, xs.at[w, 0, 0])
 
 
 def fast_body(n, nt, tiles, tile_src, tile_dst, leaf_rhs, leaf_inv, leaf_owner, anc_rhs, anc_inv, anc_owner):
@@ -202,7 +239,7 @@
     kinds = tiles.shape[2]
     ch, share, every = depth // n, count // n, n * nt
     waves = WAVES - 1
-    phases = 4 + 3 * waves
+    phases = 6 + 3 * waves
     any_spec = pl.BlockSpec(memory_space=pl.ANY)
     smem = pl.BlockSpec(memory_space=pltpu.SMEM)
     found = pl.pallas_call(
@@ -219,7 +256,8 @@
             pltpu.VMEM((n, share, depth), BF16),
             pltpu.VMEM((n, share, depth), BF16),
             pltpu.VMEM((n, WB, share, depth), BF16),
-            pltpu.VMEM((n, ch, depth), BF16),
+            pltpu.VMEM((n, ch, depth // nt), BF16),
+            pltpu.VMEM((waves, ch, depth // nt), BF16),
             pltpu.VMEM((waves, n, ch, depth), BF16),
             pltpu.VMEM((WB * waves, count, depth), BF16),
             pltpu.VMEM((waves, WB, n, share, depth), BF16),
@@ -250,7 +288,7 @@
 
     def body(*args):
         depth, count = args[3].shape[-2:]
-        if nt == WB and depth % (16 * n) == 0 and count % (8 * n) == 0:
+        if nt == WB and n > 3 and depth % (16 * n) == 0 and depth % (128 * nt) == 0 and count % (8 * n) == 0:
             return fast_body(n, nt, *args)
         return general_body(*args)
 

time: 38.5 us -> 35.4 us (0.919)
  Pallas kernels: 36.9 us -> 33.9 us
    pallas_call x1, Pallas kernels: 36.9 us -> 33.9 us  [fast_body(): pl.pallas_call(functools.partial(kernel, n, nt), out_shape=jax.ShapeDtype...]
where the time goes in v2:
time: 35.4 us; the launch traced here: 35.2 us
  Pallas kernels  33.9 us (96%)
  local copies, waits for them, and re-layouts  1.32 us (4%)
    pallas_call x1, Pallas kernels, fast_body(): pl.pallas_call(functools.partial(kernel, n, nt), out_shape=jax.ShapeDtype...  33.9 us
    unnamed x1, local copies, waits for them, and re-layouts  1.32 us

profile of v2, /device:TPU:0, one launch (start us, length us, event | category | flops | bytes accessed | tf_op | source)
XLA Modules:
  0.0 35.2 jit_solution(1741005119155509879)
XLA Ops:
  0.0 33.9 %shard_map.91 = bf16[4,8,256]{2,1,0:T(8,128)(2,1)} custom-call(bf16[1,1,4,256,256]{4,3,2,1,0:T(8,128)(2,1)} %tiles_h.1, s32[1,1,4]{2,1,0:T(1,128)} %src.1, s32[1,1,4]{2,1,0:T(1,128)} %dst.1, bf16[1,1,256,128]{3,2,1,0:T(8,128)(2,1)} %rhs_h.1, bf16[1,1,256,256]{3,2,1,0:T(8,128)(2,1)} %linv_h.1, s32[1,2]{1,0:T(1,128)} %lown.1, bf16[1,1,256,128]{3,2,1,0:T(8,128)(2,1)} %arhs_h.1, ...), custom_call_target="tpu_custom_call" | custom-call | tf_op jit(solution)/shard_map/pallas_call | solution.py:245
  33.9 1.3 %copy.11 = bf16[4,256,8]{1,2,0:T(8,128)(2,1)} copy(bf16[4,256,8]{1,2,0:T(8,128)(2,1)} %bitcast.1) | data formatting | bytes 32768

commit v3 on v2

--- a/solution.py
+++ b/solution.py
@@ -80,7 +80,11 @@
             bit *= 2
         return j
 
-    others = [partner(m) for m in range(n - 1, 0, -1)]
+    inner = 1
+    while inner * inner * 4 <= n and n % (inner * 2) == 0:
+        inner *= 2
+    masks = sorted(range(1, n), key=lambda m: (-(m // inner + m % inner), m // inner))
+    others = [partner(m) for m in masks]
     everyone = [(j, q) for j in others for q in (t, 1 - t)] + [(r, 1 - t)]
 
     barrier = pltpu.get_barrier_semaphore()
@@ -124,9 +128,6 @@
         pltpu.make_async_copy(view, view, ssem.at[phase]).wait()
 
     most = pl.ds(0, n - 1)
-    inner = 1
-    while inner * inner * 4 <= n and n % (inner * 2) == 0:
-        inner *= 2
     outer = n // inner
     ro, ri = r // inner, lax.rem(r, inner)
     chunk = ri * outer + ro

time: 35.4 us -> 35.4 us (level)
  no operation moved by 1% of the time
where the time goes in v3:
time: 35.4 us; the launch traced here: 35.1 us
  Pallas kernels  33.8 us (95%)
  local copies, waits for them, and re-layouts  1.32 us (4%)
    pallas_call x1, Pallas kernels, fast_body(): pl.pallas_call(functools.partial(kernel, n, nt), out_shape=jax.ShapeDtype...  33.8 us
    unnamed x1, local copies, waits for them, and re-layouts  1.32 us

profile of v3, /device:TPU:0, one launch (start us, length us, event | category | flops | bytes accessed | tf_op | source)
XLA Modules:
  0.0 35.1 jit_solution(16118560547811857037)
XLA Ops:
  0.0 33.8 %shard_map.91 = bf16[4,8,256]{2,1,0:T(8,128)(2,1)} custom-call(bf16[1,1,4,256,256]{4,3,2,1,0:T(8,128)(2,1)} %tiles_h.1, s32[1,1,4]{2,1,0:T(1,128)} %src.1, s32[1,1,4]{2,1,0:T(1,128)} %dst.1, bf16[1,1,256,128]{3,2,1,0:T(8,128)(2,1)} %rhs_h.1, bf16[1,1,256,256]{3,2,1,0:T(8,128)(2,1)} %linv_h.1, s32[1,2]{1,0:T(1,128)} %lown.1, bf16[1,1,256,128]{3,2,1,0:T(8,128)(2,1)} %arhs_h.1, ...), custom_call_target="tpu_custom_call" | custom-call | tf_op jit(solution)/shard_map/pallas_call | solution.py:246
  33.8 1.3 %copy.11 = bf16[4,256,8]{1,2,0:T(8,128)(2,1)} copy(bf16[4,256,8]{1,2,0:T(8,128)(2,1)} %bitcast.1) | data formatting | bytes 32768

commit v4 on v3

--- a/solution.py
+++ b/solution.py
@@ -194,7 +194,9 @@
             for k in range(TW):
                 part = part - jnp.where(dst[0, 0, w * TW + k] == b, products[k], 0.0)
             u_send[w, b] = part.reshape(n, share, depth).astype(BF16)
-        all_send(up, lambda pr, pt: (u_send.at[w, pt, pr], u_recv.at[w, r * nt + t]))
+            for j in others:
+                push(up, u_send.at[w, b, j], u_recv.at[w, r * nt + t], (j, b))
+        push(up, u_send.at[w, 1 - t, r], u_recv.at[w, r * nt + t], (r, 1 - t))
         u_recv[w, r * nt + t] = u_send[w, t, r]
         if w == 0:
             landed(3, outer_view)

time: 35.4 us -> 35.6 us (level)
  no operation moved by 1% of the time
where the time goes in v4:
time: 35.6 us; the launch traced here: 35.3 us
  Pallas kernels  34 us (96%)
  local copies, waits for them, and re-layouts  1.32 us (4%)
    pallas_call x1, Pallas kernels, fast_body(): pl.pallas_call(functools.partial(kernel, n, nt), out_shape=jax.ShapeDtype...  34 us
    unnamed x1, local copies, waits for them, and re-layouts  1.32 us

profile of v4, /device:TPU:0, one launch (start us, length us, event | category | flops | bytes accessed | tf_op | source)
XLA Modules:
  0.0 35.3 jit_solution(5347944057654236756)
XLA Ops:
  0.0 34.0 %shard_map.91 = bf16[4,8,256]{2,1,0:T(8,128)(2,1)} custom-call(bf16[1,1,4,256,256]{4,3,2,1,0:T(8,128)(2,1)} %tiles_h.1, s32[1,1,4]{2,1,0:T(1,128)} %src.1, s32[1,1,4]{2,1,0:T(1,128)} %dst.1, bf16[1,1,256,128]{3,2,1,0:T(8,128)(2,1)} %rhs_h.1, bf16[1,1,256,256]{3,2,1,0:T(8,128)(2,1)} %linv_h.1, s32[1,2]{1,0:T(1,128)} %lown.1, bf16[1,1,256,128]{3,2,1,0:T(8,128)(2,1)} %arhs_h.1, ...), custom_call_target="tpu_custom_call" | custom-call | tf_op jit(solution)/shard_map/pallas_call | solution.py:248
  34.0 1.3 %copy.11 = bf16[4,256,8]{1,2,0:T(8,128)(2,1)} copy(bf16[4,256,8]{1,2,0:T(8,128)(2,1)} %bitcast.1) | data formatting | bytes 32768
